TPU v7x, 32 devices: a whole 2x2x4 slice. The times are simulated.
32 devices in a mesh: dp: 4 (over y, x), tensor: 8 (over z, core).
Axes of the slice: x: 2, y: 2, z: 4, core: 2. Of those that a mesh axis runs over, the one named last changes fastest.
Arguments:
- hidden_act: bfloat16 [2816, 36864], P('dp', 'tensor'), may hold values from -80 to 80
- out_grad: bfloat16 [2816, 4608], P('dp', 'tensor'), may hold values from -0.5 to 0.5
- other_sq: float32 [8], P('dp'), may hold values from 2989699 to 597939968
Outputs:
- weight_grad: float32 [4608, 36864], P('dp', 'tensor')
All inputs are finite; a program needn't handle non-finite values.
Results may differ from a plain program's by a relative error of at most 0.002.
Values may be sent and summed in bfloat16 or wider, within the bound.
No kernel may reach another device: no remote copies, remote signals or barrier semaphores. Data moves between devices by JAX's collectives and lax.ppermute only.
A program may use at most 128 MiB of HBM per device.

v0:
```python
import math
import jax
import jax.numpy as jnp
from jax import lax
from jax.sharding import PartitionSpec as P

D = 4608
FF = 36864
L = 352


def on_device(hidden_act, out_grad, other_sq):
    examples_here = other_sq.shape[0]
    length = hidden_act.shape[0] // examples_here
    hidden_blocks = hidden_act.reshape(examples_here, length, hidden_act.shape[1])
    act_gram = jnp.einsum(
        "etf,esf->ets", hidden_blocks, hidden_blocks, preferred_element_type=jnp.float32
    )
    full_grad = lax.all_gather(out_grad, "tensor", axis=1, tiled=True)
    grad_blocks = full_grad.reshape(examples_here, length, full_grad.shape[1])
    local_blocks = out_grad.reshape(examples_here, length, out_grad.shape[1])
    grad_part = jnp.einsum(
        "etd,esd->ets", local_blocks, local_blocks, preferred_element_type=jnp.float32
    )
    act_total, grad_total = lax.psum((act_gram, grad_part), "tensor")
    layer_sq = jnp.sum(act_total * grad_total, axis=(1, 2))
    clip_bound = math.sqrt(L * FF * D / 80.0)
    clip_scale = jnp.minimum(1.0, clip_bound / jnp.sqrt(other_sq + layer_sq))
    scaled_grad = (grad_blocks.astype(jnp.float32) * clip_scale[:, None, None]).astype(jnp.bfloat16)
    scaled_grad = scaled_grad.reshape(examples_here * length, full_grad.shape[1])
    contract_rows = (((0,), (0,)), ((), ()))
    own_columns = lax.all_to_all(scaled_grad, "dp", split_axis=1, concat_axis=0, tiled=True)
    return lax.dot_general(
        own_columns,
        lax.all_gather(hidden_act, "dp", axis=0, tiled=True),
        contract_rows,
        preferred_element_type=jnp.float32,
    )


def solution(mesh):
    placed = (P("dp", "tensor"), P("dp", "tensor"), P("dp"))
    return jax.shard_map(
        on_device, mesh=mesh, in_specs=placed, out_specs=P("dp", "tensor"), check_vma=False
    )
```

profile of v0, /device:TPU:0, one launch (start us, length us, event | category | flops | bytes accessed | tf_op | source)
XLA Modules:
  0.0 509.5 jit_solution(13923911477526798754)
XLA Ops:
  6.5 0.0 all-reduce.3.cloned.1.call-start
  6.5 2.6 reshape.14
  9.2 1.7 fusion
  10.9 9.2 %fusion.2 = f32[2,352,352]{2,1,0:T(8,128)} fusion(bf16[2,352,4608]{2,1,0:T(8,128)(2,1)} %bitcast.16), kind=kOutput, calls=%fused_computation.6 | convolution fusion | flops 2283798528 | bytes 7479296 | tf_op jit(solution)/shard_map/etf,esf->ets/dot_general | solution.py:16
  20.1 0.0 copy-start
  20.1 0.0 all-reduce.3.cloned.1.call-update
  20.1 0.0 all-gather.3.cloned.1.call-start
  20.2 0.7 all-gather.3.cloned.1.call-update
  20.9 0.0 all-gather.5.cloned.1.call-start
  20.9 0.7 all-gather.5.cloned.1.call-update
  21.6 67.1 %all-reduce.3.cloned.1.call-done = (f32[2,352,352]{2,1,0:T(8,128)}, f32[2,352,352]{2,1,0:T(8,128)}) async-done(((f32[2,352,352]{2,1,0:T(8,128)}, f32[2,352,352]{2,1,0:T(8,128)}), (f32[2,352,352]{2,1,0:T(8,128)}, f32[2,352,352]{2,1,0:T(8,128)})) %all-reduce.3.cloned.1.call-update) | async-done | bytes 1982480 | tf_op jit(solution)/shard_map/psum | solution.py:25
  88.7 1.8 multiply_reduce_fusion
  90.5 0.0 copy-done
  90.5 0.1 mul.17
  90.6 0.1 mul.18
  90.7 70.5 %all-gather.3.cloned.1.call-done = bf16[704,4608]{0,1:T(8,128)(2,1)} async-done(((bf16[704,576]{0,1:T(8,128)(2,1)}), bf16[704,4608]{0,1:T(8,128)(2,1)}) %all-gather.3.cloned.1.call-update) | async-done | bytes 6488080 | tf_op jit(solution)/shard_map/all_gather | solution.py:19
  161.1 10.0 %copy.20 = bf16[704,4608]{1,0:T(8,128)(2,1)} copy(bf16[704,4608]{0,1:T(8,128)(2,1)} %all-gather.3.cloned.1.call-done) | data formatting | bytes 12976128 | tf_op jit(solution)/shard_map/all_gather | solution.py:19
  171.2 6.6 %multiply_convert_fusion = bf16[704,4608]{1,0:T(8,128)(2,1)S(1)} fusion(bf16[704,4608]{1,0:T(8,128)(2,1)} %copy.20, f32[704]{0:T(1024)S(1)} %mul.18), kind=kLoop, calls=%fused_computation | loop fusion | flops 9732096 | bytes 12978944 | tf_op jit(solution)/shard_map/convert_element_type | solution.py:29
  177.7 0.5 copy.28
  178.2 140.2 %all_to_all.19 = bf16[704,4,1152]{2,0,1:T(8,128)(2,1)} all-to-all(bf16[704,4,1152]{2,0,1:T(8,128)(2,1)S(1)} %bitcast.15), channel_id=1, replica_groups=mesh['dp'=4,'tensor'=8] {'dp'}, dimensions={1} | all-to-all | bytes 12976128 | tf_op jit(solution)/shard_map/all_to_all | solution.py:32
  318.4 146.8 %all-gather.5.cloned.1.call-done = bf16[2816,4608]{1,0:T(8,128)(2,1)} async-done(((bf16[704,4608]{1,0:T(8,128)(2,1)}), bf16[2816,4608]{1,0:T(8,128)(2,1)}) %all-gather.5.cloned.1.call-update) | async-done | bytes 25952272 | tf_op jit(solution)/shard_map/all_gather | solution.py:35
  465.2 37.7 %fusion.3 = f32[1152,4608]{1,0:T(8,128)} fusion(bf16[2816,1152]{1,0:T(8,128)(2,1)} %bitcast.17, bf16[2816,4608]{1,0:T(8,128)(2,1)} %all-gather.5.cloned.1.call-done), kind=kOutput, calls=%fused_computation.7 | convolution fusion | flops 29896998912 | bytes 53673984 | tf_op jit(solution)/shard_map/dot_general | solution.py:33
  (1 shorter events, 0.0 us)
Async XLA Ops:
  6.5 82.2 %all-reduce.3.cloned.1.call-start = ((), (), s32[]{:S(2)}) async-start(), calls=%async_computation.3 | async-start | bytes 4325376 | tf_op jit(solution)/shard_map/psum | solution.py:25
  20.1 70.4 %copy-start = (f32[2]{0:T(128)S(1)}, f32[2]{0:T(128)}, u32[]{:S(2)}) copy-start(f32[2]{0:T(128)} %param.5) | copy-start | bytes 28
  20.1 141.0 %all-gather.3.cloned.1.call-start = ((), (), s32[]{:S(2)}) async-start(), calls=%async_computation.1 | async-start | bytes 7962624 | tf_op jit(solution)/shard_map/all_gather | solution.py:19
  20.9 444.3 %all-gather.5.cloned.1.call-start = ((), (), s32[]{:S(2)}) async-start(), calls=%async_computation.2 | async-start | bytes 32440320 | tf_op jit(solution)/shard_map/all_gather | solution.py:35
Sparse Core Ops, SparseCore 0:
  20.2 68.4 all-reduce.2
  90.3 70.7 all-gather.2
  163.0 302.1 all-gather.4
where the time goes:
time: 510 us; the launch traced here: 509 us
  waiting for transfers between devices  286 us (56%)
  blocking collectives  140 us (27%)
  matrix products  48.6 us (10%)
  local copies, waits for them, and re-layouts  13.3 us (3%)
  between operations  13.1 us (3%)
  other arithmetic  8.38 us (2%)
    all_gather x1, waiting for transfers between devices, on_device(): lax.all_gather(hidden_act, 'dp', axis=0, tiled=True)  147 us
    all_to_all x1, blocking collectives, on_device(): lax.all_to_all(scaled_grad, 'dp', split_axis=1, concat_axis=0, tiled=True)  140 us
    all_gather x1, waiting for transfers between devices, on_device(): full_grad = lax.all_gather(out_grad, 'tensor', axis=1, tiled=True)  70.5 us
    psum x1, waiting for transfers between devices, on_device(): act_total, grad_total = lax.psum((act_gram, grad_part), 'tensor')  67.1 us
    dot_general x1, matrix products, on_device(): lax.dot_general(own_columns, lax.all_gather(hidden_act, 'dp', axis=0, til...  37.7 us
  transfers between devices with their start and end apart: 3, of which 3 were waited for; matrix products, arithmetic and copies ran while one was open for 4% of the time, Pallas kernels for 0%

commit v1 on v0

--- a/solution.py
+++ b/solution.py
@@ -16,7 +16,15 @@
     act_gram = jnp.einsum(
         "etf,esf->ets", hidden_blocks, hidden_blocks, preferred_element_type=jnp.float32
     )
-    full_grad = lax.all_gather(out_grad, "tensor", axis=1, tiled=True)
+    ways, here = (lax.axis_size("tensor"), lax.axis_index("tensor"))
+    grown, reach = (out_grad, 1)
+    while reach < ways:
+        theirs = lax.ppermute(grown, "tensor", [(d, d ^ reach) for d in range(ways)])
+        mine_first = jnp.concatenate([grown, theirs], axis=1)
+        theirs_first = jnp.concatenate([theirs, grown], axis=1)
+        grown = jnp.where(here & reach == 0, mine_first, theirs_first)
+        reach = 2 * reach
+    full_grad = grown
     grad_blocks = full_grad.reshape(examples_here, length, full_grad.shape[1])
     local_blocks = out_grad.reshape(examples_here, length, out_grad.shape[1])
     grad_part = jnp.einsum(

time: 510 us -> 376 us (0.74)
  waiting for transfers between devices: 286 us -> 206 us
  blocking collectives: 140 us -> 78.2 us
  starting transfers between devices: 0.08 us -> 5.97 us
    all_gather x1, waiting for transfers between devices: 147 us -> 0.01 us  [on_device(): lax.all_gather(hidden_act, 'dp', axis=0, tiled=True)]
    ppermute x0 -> x3, waiting for transfers between devices: none -> 123 us  [on_device(): lax.ppermute(grown, 'tensor', [(d, d ^ reach) for d in range(ways)])]
    all_gather x1 -> x0, waiting for transfers between devices: 70.5 us -> none  [on_device(): full_grad = lax.all_gather(out_grad, 'tensor', axis=1, tiled=True)]
    all_to_all x1, blocking collectives: 140 us -> 78.2 us  [on_device(): lax.all_to_all(scaled_grad, 'dp', split_axis=1, concat_axis=0, tiled=True)]
    psum x1, waiting for transfers between devices: 67.1 us -> 82.3 us  [on_device(): act_total, grad_total = lax.psum((act_gram, grad_part), 'tensor')]
    all_gather x1 -> x0, local copies, waits for them, and re-layouts: 10 us -> none  [on_device(): full_grad = lax.all_gather(out_grad, 'tensor', axis=1, tiled=True)]
    select_n x0 -> x4, other arithmetic: none -> 9.07 us  [on_device(): grown = jnp.where(here & reach == 0, mine_first, theirs_first)]
    ppermute x0 -> x3, starting transfers between devices: none -> 5.93 us  [on_device(): lax.ppermute(grown, 'tensor', [(d, d ^ reach) for d in range(ways)])]
  transfers between devices with their start and end apart: 3 -> 5, of which waited for: 3 -> 4; matrix products, arithmetic and copies ran while one was open for 4% -> 5% of each run, Pallas kernels for 0% -> 0%
where the time goes in v1:
time: 376 us; the launch traced here: 375 us
  waiting for transfers between devices  206 us (55%)
  blocking collectives  78.2 us (21%)
  matrix products  48.7 us (13%)
  between operations  14.9 us (4%)
  other arithmetic  13.2 us (4%)
  local copies, waits for them, and re-layouts  8.41 us (2%)
  starting transfers between devices  5.97 us (2%)
    ppermute x3, waiting for transfers between devices, on_device(): lax.ppermute(grown, 'tensor', [(d, d ^ reach) for d in range(ways)])  123 us
    psum x1, waiting for transfers between devices, on_device(): act_total, grad_total = lax.psum((act_gram, grad_part), 'tensor')  82.3 us
    all_to_all x1, blocking collectives, on_device(): lax.all_to_all(scaled_grad, 'dp', split_axis=1, concat_axis=0, tiled=True)  78.2 us
    dot_general x1, matrix products, on_device(): lax.dot_general(own_columns, lax.all_gather(hidden_act, 'dp', axis=0, til...  37.7 us
    dot_general x1, matrix products, on_device(): jnp.einsum('etf,esf->ets', hidden_blocks, hidden_blocks, preferred_elemen...  9.23 us
    select_n x4, other arithmetic, on_device(): grown = jnp.where(here & reach == 0, mine_first, theirs_first)  9.07 us
  transfers between devices with their start and end apart: 5, of which 4 were waited for; matrix products, arithmetic and copies ran while one was open for 5% of the time, Pallas kernels for 0%

profile of v1, /device:TPU:0, one launch (start us, length us, event | category | flops | bytes accessed | tf_op | source)
XLA Modules:
  0.0 375.3 jit_solution(245679214048294830)
XLA Ops:
  7.4 2.6 reshape.64
  10.0 1.7 fusion
  11.7 9.2 %fusion.2 = f32[2,352,352]{2,1,0:T(8,128)} fusion(bf16[2,352,4608]{2,1,0:T(8,128)(2,1)} %bitcast.20), kind=kOutput, calls=%fused_computation.11 | convolution fusion | flops 2283798528 | bytes 7479296 | tf_op jit(solution)/shard_map/etf,esf->ets/dot_general | solution.py:16
  21.1 0.5 all-gather.2.cloned.1.call-update
  21.6 0.6 copy-done.1
  22.2 0.5 collective-permute-start
  22.7 1.0 copy.29
  23.7 1.2 collective-permute-done
  24.9 1.9 copy.30
  26.7 2.3 maximum_select_fusion.4
  29.1 2.9 collective-permute-start.1
  32.0 61.2 %collective-permute-done.1 = bf16[704,1152]{1,0:T(8,128)(2,1)S(1)} collective-permute-done((bf16[704,1152]{1,0:T(8,128)(2,1)}, bf16[704,1152]{1,0:T(8,128)(2,1)S(1)}, u32[]{:S(2)}, u32[]{:S(2)}) %collective-permute-start.1) | collective-permute-done | bytes 1622048 | tf_op jit(solution)/shard_map/ppermute | solution.py:22
  93.2 3.8 %maximum_select_fusion.2 = bf16[704,2304]{1,0:T(8,128)(2,1)} fusion(bf16[704,1152]{1,0:T(8,128)(2,1)S(1)} %collective-permute-done.1, bf16[704,1152]{1,0:T(8,128)(2,1)} %maximum_select_fusion.4, pred[]{:T(512)S(6)} %eq.10), kind=kLoop, calls=%fused_computation.4 | loop fusion | flops 14598144 | bytes 6488065 | tf_op jit(solution)/shard_map/jit(_where)/select_n | solution.py:25
  97.0 2.5 collective-permute-start.2
  99.5 2.4 maximum_select_fusion.3
  101.9 82.3 %all-reduce.3.cloned.1.call-done = (f32[2,352,352]{2,1,0:T(8,128)}, f32[2,352,352]{2,1,0:T(8,128)}) async-done(((f32[2,352,352]{2,1,0:T(8,128)}, f32[2,352,352]{2,1,0:T(8,128)}), (f32[2,352,352]{2,1,0:T(8,128)}, f32[2,352,352]{2,1,0:T(8,128)})) %all-reduce.3.cloned.1.call-update) | async-done | bytes 1982480 | tf_op jit(solution)/shard_map/psum | solution.py:33
  184.2 1.8 multiply_reduce_fusion
  186.1 0.1 mul.19
  186.2 0.6 maximum_select_fusion.1
  186.8 60.7 %collective-permute-done.2 = bf16[704,2304]{1,0:T(8,128)(2,1)} collective-permute-done((bf16[704,2304]{1,0:T(8,128)(2,1)}, bf16[704,2304]{1,0:T(8,128)(2,1)}, u32[]{:S(2)}, u32[]{:S(2)}) %collective-permute-start.2) | collective-permute-done | bytes 3244064 | tf_op jit(solution)/shard_map/ppermute | solution.py:22
  247.5 2.2 copy.43
  249.6 2.3 multiply_convert_fusion
  251.9 78.2 %all_to_all.16 = bf16[704,4,1152]{2,0,1:T(8,128)(2,1)} all-to-all(bf16[704,4,1152]{2,0,1:T(8,128)(2,1)S(1)} %multiply_convert_fusion), channel_id=1, replica_groups=mesh['dp'=4,'tensor'=8] {'dp'}, dimensions={1} | all-to-all | bytes 12976128 | tf_op jit(solution)/shard_map/all_to_all | solution.py:40
  330.2 37.7 %fusion.3 = f32[1152,4608]{1,0:T(8,128)} fusion(bf16[2816,1152]{1,0:T(8,128)(2,1)} %bitcast.21, bf16[2816,4608]{1,0:T(8,128)(2,1)} %all-gather.2.cloned.1.call-done), kind=kOutput, calls=%fused_computation.12 | convolution fusion | flops 29896998912 | bytes 53673984 | tf_op jit(solution)/shard_map/dot_general | solution.py:41
  (11 shorter events, 0.2 us)
Async XLA Ops:
  7.4 176.8 %all-reduce.3.cloned.1.call-start = ((), (), s32[]{:S(2)}) async-start(), calls=%async_computation.2 | async-start | bytes 4325376 | tf_op jit(solution)/shard_map/psum | solution.py:33
  21.0 1.2 copy-start.1
  21.0 309.1 %all-gather.2.cloned.1.call-start = ((), (), s32[]{:S(2)}) async-start(), calls=%async_computation.1 | async-start | bytes 32440320 | tf_op jit(solution)/shard_map/all_gather | solution.py:43
  22.2 2.7 collective-permute-start
  29.1 64.1 %collective-permute-start.1 = (bf16[704,1152]{1,0:T(8,128)(2,1)}, bf16[704,1152]{1,0:T(8,128)(2,1)S(1)}, u32[]{:S(2)}, u32[]{:S(2)}) collective-permute-start(bf16[704,1152]{1,0:T(8,128)(2,1)} %maximum_select_fusion.4), channel_id=1, source_target_pairs={{0,2},{1,3},{2,0},{3,1},{4,6},{5,7},{6,4},{7,5},{8,10},{9,11},{10,... | collective-permute-start | bytes 4866056 | tf_op jit(solution)/shard_map/ppermute | solution.py:22
  97.0 89.0 %copy-start.2 = (f32[2]{0:T(128)S(1)}, f32[2]{0:T(128)}, u32[]{:S(2)}) copy-start(f32[2]{0:T(128)} %param.5) | copy-start | bytes 28
  97.0 150.5 %collective-permute-start.2 = (bf16[704,2304]{1,0:T(8,128)(2,1)}, bf16[704,2304]{1,0:T(8,128)(2,1)}, u32[]{:S(2)}, u32[]{:S(2)}) collective-permute-start(bf16[704,2304]{1,0:T(8,128)(2,1)} %maximum_select_fusion.2), channel_id=1, source_target_pairs={{0,4},{1,5},{2,6},{3,7},{4,0},{5,1},{6,2},{7,3},{8,12},{9,13},{10,... | collective-permute-start | bytes 9732104 | tf_op jit(solution)/shard_map/ppermute | solution.py:22
  101.9 84.3 %copy-start = (bf16[704,1,1152]{2,0,1:T(8,128)(2,1)S(1)}, bf16[704,1,1152]{2,0,1:T(8,128)(2,1)}, u32[]{:S(2)}) copy-start(bf16[704,1,1152]{2,0,1:T(8,128)(2,1)} %maximum_select_fusion.3) | copy-start | bytes 4866052
Sparse Core Ops, SparseCore 0:
  21.1 163.0 all-reduce.2
Sparse Core Ops, SparseCore 1:
  23.4 239.4 all-gather.1
